TPU v7x, 256 devices: a whole 4x4x8 slice. The times are simulated.
256 devices in a mesh: scen: 16 (over z, core), clus: 16 (over y, x).
Axes of the slice: x: 4, y: 4, z: 8, core: 2. Of those that a mesh axis runs over, the one named last changes fastest.
Arguments:
- duals: bfloat16 [16384, 2, 128], P(('scen', 'clus')), may hold values from -6 to 6
- blocks: bfloat16 [16384, 2, 128, 128], P(('scen', 'clus')), may hold values from -0.5 to 0.5
- prob: float32 [16384], P(('scen', 'clus')), may hold values from 0.25 to 4
- cluster_map: int32 [16384], P(('scen', 'clus')), may hold values from 0 to 15
- block_cols: int32 [16384, 2], P(('scen', 'clus')), may hold values from 0 to 255
- counts: int32 [256], P(('scen', 'clus')), may hold values from 16 to 64, as said below
- cut_owner_rows: int32 [256], replicated, may hold values from 0 to 255, as said below
Outputs:
- master_cuts: float32 [256, 32768], P('clus', 'scen')
Inputs may be any that keep to these rules, and one draw needn't show every extreme that they name: counts of live slots, one device holding 64 live slots in every draw. A permutation of the master cut rows; of the cuts k = i * 16 to (i + 1) * 16 - 1 at most 1 have cut_owner_rows[k] in e * 16 to (e + 1) * 16 - 1, for any i and e, and 1 is reached.
All inputs are finite; a program needn't handle non-finite values.
Results may differ from a plain program's by a relative error of at most 0.0029.
Values sent between devices are 32-bit elements; how exact they have to be, the bound alone decides.
A program may use at most 64 MiB of HBM per device.

v0:
```python
import jax
import jax.numpy as jnp
from jax import lax
from jax.sharding import PartitionSpec as P

N1 = 32768
KC = 16


def body(duals, blocks, prob, cluster_map, block_cols, counts, cut_owner_rows):
    slots = prob.shape[0]
    width = blocks.shape[-1]
    col_blocks = N1 // width
    cluster_position = lax.axis_index("clus")
    own_blocks = col_blocks // lax.axis_size("scen")
    columns = own_blocks * width
    live = jnp.arange(slots, dtype=jnp.int32) < counts[0]
    weight = jnp.where(live, prob, jnp.float32(0.0))
    weighted_duals = (weight[:, None, None] * duals.astype(jnp.float32)).astype(jnp.bfloat16)
    dual_products = jnp.einsum(
        "plqv,plq->plv", blocks, weighted_duals, preferred_element_type=jnp.float32
    )
    dual_products = dual_products.reshape(-1, width)
    keys = (cluster_map[:, None] * col_blocks + block_cols).reshape(-1)
    clus_part = keys // col_blocks
    col_part = keys % col_blocks
    valid = (col_part >= 0) & (col_part < lax.axis_size("scen") * own_blocks)
    target = jnp.where(valid, col_part * KC + clus_part, -1)
    onehot = (
        target[None, :]
        == jnp.arange(lax.axis_size("scen") * own_blocks * KC, dtype=jnp.int32)[:, None]
    ).astype(jnp.float32)
    summed = jnp.dot(
        onehot, dual_products, precision=lax.Precision.HIGHEST, preferred_element_type=jnp.float32
    )
    probability_shares = lax.psum_scatter(
        summed.reshape(lax.axis_size("scen") * own_blocks, KC, width),
        "scen",
        scatter_dimension=0,
        tiled=True,
    )
    reduced = jnp.transpose(probability_shares, (1, 0, 2)).reshape(KC, columns)
    owners = cut_owner_rows - cluster_position * KC
    onehot = (owners[None, :] == jnp.arange(KC, dtype=jnp.int32)[:, None]).astype(jnp.float32)
    return jnp.dot(
        onehot,
        lax.all_gather(reduced, "clus", axis=0, tiled=True),
        precision=lax.Precision.HIGHEST,
        preferred_element_type=jnp.float32,
    )


def solution(mesh):
    placed = (
        P(("scen", "clus"), None, None),
        P(("scen", "clus"), None, None, None),
        P(("scen", "clus")),
        P(("scen", "clus")),
        P(("scen", "clus"), None),
        P(("scen", "clus")),
        P(),
    )
    return jax.shard_map(
        body, mesh=mesh, in_specs=placed, out_specs=P("clus", "scen"), check_vma=False
    )
```

profile of v0, /device:TPU:1, one launch (start us, length us, event | category | flops | bytes accessed | tf_op | source)
XLA Modules:
  0.0 139.5 jit_solution(1167170672462910426)
XLA Ops:
  6.5 0.0 reduce-scatter.2.cloned.1.call-start
  7.2 0.7 broadcast_multiply_fusion
  7.9 0.7 broadcast_add_fusion
  8.5 0.1 copy.9
  8.6 0.1 reshape.86
  8.8 0.7 compare_select_fusion
  9.5 0.9 fusion.6
  10.3 3.4 %fusion.4 = f32[64,2,1,128]{3,2,1,0:T(1,128)S(1)} fusion(bf16[64,2,128,128]{3,2,1,0:T(8,128)(2,1)} %param.8, bf16[64,2,128,1]{2,1,0,3:T(2,128)(2,1)S(1)} %fusion.6), kind=kOutput, calls=%fused_computation.5 | convolution fusion | flops 4194304 | bytes 4292608 | tf_op jit(solution)/shard_map/plqv,plq->plv/dot_general | solution.py:20
  13.7 0.0 copy-start
  13.7 2.5 %fusion = f32[256,16,128]{2,0,1:T(8,128)} fusion(f32[128,128,1]{1,0,2:T(8,128)S(1)} %bitcast.19, s32[256,16]{0,1:T(8,128)S(1)} %multiply_add_fusion, s32[128]{0:T(128)S(1)} %and_select_fusion.1), kind=kOutput, calls=%fused_computation | convolution fusion | flops 805830656 | bytes 2179584 | tf_op jit(solution)/shard_map/dot_general | solution.py:33
  16.2 0.0 reduce-scatter.2.cloned.1.call-update
  16.3 0.0 all-gather.2.cloned.1.call-start
  16.3 60.2 %reduce-scatter.2.cloned.1.call-done = f32[16,16,128]{2,0,1:T(8,128)} async-done(((f32[256,16,128]{2,0,1:T(8,128)}), f32[16,16,128]{2,0,1:T(8,128)}) %reduce-scatter.2.cloned.1.call-update) | async-done | bytes 131088 | tf_op jit(solution)/shard_map/reduce_scatter | solution.py:36
  76.6 1.6 %copy.16 = f32[2,8,16,128]{3,1,2,0:T(8,128)} copy(f32[2,8,16,128]{3,2,1,0:T(8,128)} %bitcast.20) | data formatting | bytes 262144
  78.2 0.0 all-gather.2.cloned.1.call-update
  78.2 0.0 copy-done
  78.2 51.4 %all-gather.2.cloned.1.call-done = f32[256,2048]{1,0:T(8,128)} async-done(((f32[16,2048]{1,0:T(8,128)}), f32[256,2048]{1,0:T(8,128)}) %all-gather.2.cloned.1.call-update) | async-done | bytes 2097168 | tf_op jit(solution)/shard_map/all_gather | solution.py:47
  129.6 3.0 %fusion.7 = f32[16,2048]{1,0:T(8,128)} fusion(f32[256,2048]{1,0:T(8,128)} %all-gather.2.cloned.1.call-done, s32[256]{0:T(256)S(1)} %broadcast_subtract_fusion), kind=kOutput, calls=%fused_computation.11 | convolution fusion | flops 100667392 | bytes 2229248 | tf_op jit(solution)/shard_map/dot_general | solution.py:45
  (3 shorter events, 0.0 us)
Async XLA Ops:
  6.5 70.0 %reduce-scatter.2.cloned.1.call-start = ((), (), s32[]{:S(2)}) async-start(), calls=%async_computation.1 | async-start | bytes 2228224 | tf_op jit(solution)/shard_map/reduce_scatter | solution.py:36
  13.7 64.5 %copy-start = (s32[256]{0:T(256)S(1)}, s32[256]{0:T(256)}, u32[]{:S(2)}) copy-start(s32[256]{0:T(256)} %param.13) | copy-start | bytes 3076
  16.3 113.3 %all-gather.2.cloned.1.call-start = ((), (), s32[]{:S(2)}) async-start(), calls=%async_computation.2 | async-start | bytes 2228224 | tf_op jit(solution)/shard_map/all_gather | solution.py:47
Sparse Core Ops, SparseCore 0:
  16.4 60.1 reduce-scatter.1
  79.0 50.5 all-gather.1
where the time goes:
time: 140 us; the launch traced here: 139 us
  waiting for transfers between devices  112 us (80%)
  between operations  14.1 us (10%)
  matrix products  8.91 us (6%)
  other arithmetic  2.91 us (2%)
  local copies, waits for them, and re-layouts  1.84 us (1%)
    reduce_scatter x1, waiting for transfers between devices, body(): lax.psum_scatter(summed.reshape(lax.axis_size('scen') * own_blocks, KC, w...  60.2 us
    all_gather x1, waiting for transfers between devices, body(): lax.all_gather(reduced, 'clus', axis=0, tiled=True)  51.4 us
    dot_general x1, matrix products, body(): jnp.einsum('plqv,plq->plv', blocks, weighted_duals, preferred_element_typ...  3.37 us
    dot_general x1, matrix products, body(): jnp.dot(onehot, lax.all_gather(reduced, 'clus', axis=0, tiled=True), prec...  3.02 us
  transfers between devices with their start and end apart: 2, of which 2 were waited for; matrix products, arithmetic and copies ran while one was open for 0% of the time, Pallas kernels for 0%

commit v1 on v0

--- a/solution.py
+++ b/solution.py
@@ -8,6 +8,28 @@
 
 
 def body(duals, blocks, prob, cluster_map, block_cols, counts, cut_owner_rows):
+
+    def keep_up_sheet(point):
+        a_name = "clus"
+        spare, formed, reply = (lax.axis_size(a_name), lax.axis_index(a_name), point.shape[0])
+        tray = [(ix, (ix + 1) % spare) for ix in range(spare)]
+        leaves = [(ix, (ix - 1) % spare) for ix in range(spare)]
+        arr_now = jnp.zeros((*point.shape[:0], spare * reply, *point.shape[1:]), point.dtype)
+        arr_now = lax.dynamic_update_slice_in_dim(arr_now, point, formed * reply, axis=0)
+        a_now = block_now = point
+        f_next = spare // 2
+        for dev in range(1, f_next + 1):
+            a_now = lax.ppermute(a_now, a_name, tray)
+            arr_now = lax.dynamic_update_slice_in_dim(
+                arr_now, a_now, (formed - dev) % spare * reply, axis=0
+            )
+            if dev < spare - f_next:
+                block_now = lax.ppermute(block_now, a_name, leaves)
+                arr_now = lax.dynamic_update_slice_in_dim(
+                    arr_now, block_now, (formed + dev) % spare * reply, axis=0
+                )
+        return arr_now
+
     slots = prob.shape[0]
     width = blocks.shape[-1]
     col_blocks = N1 // width
@@ -44,7 +66,7 @@
     onehot = (owners[None, :] == jnp.arange(KC, dtype=jnp.int32)[:, None]).astype(jnp.float32)
     return jnp.dot(
         onehot,
-        lax.all_gather(reduced, "clus", axis=0, tiled=True),
+        keep_up_sheet(reduced),
         precision=lax.Precision.HIGHEST,
         preferred_element_type=jnp.float32,
     )

time: 140 us -> 155 us (1.11)
  the two profiles are of different devices: /device:TPU:1 before, /device:TPU:0 now
where the time goes in v1:
time: 155 us; the launch traced here: 154 us
  waiting for transfers between devices  90.2 us (58%)
  starting transfers between devices  37.8 us (24%)
  between operations  14.5 us (9%)
  matrix products  7.28 us (5%)
  other arithmetic  2.92 us (2%)
  local copies, waits for them, and re-layouts  1.75 us (1%)
    reduce_scatter x1, waiting for transfers between devices, body(): lax.psum_scatter(summed.reshape(lax.axis_size('scen') * own_blocks, KC, w...  60.4 us
    ppermute x7, starting transfers between devices, keep_up_sheet(): block_now = lax.ppermute(block_now, a_name, leaves)  36.2 us
    ppermute x8, waiting for transfers between devices, keep_up_sheet(): a_now = lax.ppermute(a_now, a_name, tray)  29.8 us
    dot_general x1, matrix products, body(): jnp.einsum('plqv,plq->plv', blocks, weighted_duals, preferred_element_typ...  3.37 us
  transfers between devices with their start and end apart: 16, of which 9 were waited for; matrix products, arithmetic and copies ran while one was open for 0% of the time, Pallas kernels for 0%

profile of v1, /device:TPU:0, one launch (start us, length us, event | category | flops | bytes accessed | tf_op | source)
XLA Modules:
  0.0 154.5 jit_solution(16136221652915514209)
XLA Ops:
  6.5 0.0 reduce-scatter.2.cloned.1.call-start
  7.2 0.7 broadcast_multiply_fusion
  7.9 0.7 broadcast_add_fusion
  8.5 0.1 copy.9
  8.6 0.1 reshape.86
  8.8 0.7 compare_select_fusion
  9.5 0.9 fusion.6
  10.3 3.4 %fusion.4 = f32[64,2,1,128]{3,2,1,0:T(1,128)S(1)} fusion(bf16[64,2,128,128]{3,2,1,0:T(8,128)(2,1)} %param.8, bf16[64,2,128,1]{2,1,0,3:T(2,128)(2,1)S(1)} %fusion.6), kind=kOutput, calls=%fused_computation.5 | convolution fusion | flops 4194304 | bytes 4292608 | tf_op jit(solution)/shard_map/plqv,plq->plv/dot_general | solution.py:42
  13.7 0.0 copy-start.1
  13.7 2.5 %fusion = f32[256,16,128]{2,0,1:T(8,128)} fusion(f32[128,128,1]{1,0,2:T(8,128)S(1)} %bitcast.22, s32[256,16]{0,1:T(8,128)S(1)} %multiply_add_fusion, s32[128]{0:T(128)S(1)} %and_select_fusion.1), kind=kOutput, calls=%fused_computation | convolution fusion | flops 805830656 | bytes 2179584 | tf_op jit(solution)/shard_map/dot_general | solution.py:55
  16.2 0.0 reduce-scatter.2.cloned.1.call-update
  16.5 0.0 copy-done.1
  16.5 60.4 %reduce-scatter.2.cloned.1.call-done = f32[16,16,128]{2,0,1:T(8,128)} async-done(((f32[256,16,128]{2,0,1:T(8,128)}), f32[16,16,128]{2,0,1:T(8,128)}) %reduce-scatter.2.cloned.1.call-update) | async-done | bytes 131088 | tf_op jit(solution)/shard_map/reduce_scatter | solution.py:58
  76.9 0.0 copy-start
  76.9 1.0 copy.18
  77.9 1.6 %collective-permute-start = (f32[16,2048]{1,0:T(8,128)S(1)}, f32[16,2048]{1,0:T(8,128)S(1)}, u32[]{:S(2)}, u32[]{:S(2)}) collective-permute-start(f32[16,2048]{1,0:T(8,128)S(1)} %bitcast.23), channel_id=1, source_target_pairs={{0,1},{1,2},{2,3},{3,4},{4,5},{5,6},{6,7},{7,8},{8,9},{9,10},{10,1... | collective-permute-start | bytes 393224 | tf_op jit(solution)/shard_map/ppermute | solution.py:22
  79.5 3.9 %collective-permute-start.1 = (f32[16,2048]{1,0:T(8,128)S(1)}, f32[16,2048]{1,0:T(8,128)S(1)}, u32[]{:S(2)}, u32[]{:S(2)}) collective-permute-start(f32[16,2048]{1,0:T(8,128)S(1)} %bitcast.24), channel_id=1, source_target_pairs={{0,15},{1,0},{2,1},{3,2},{4,3},{5,4},{6,5},{7,6},{8,7},{9,8},{10,9... | collective-permute-start | bytes 393224 | tf_op jit(solution)/shard_map/ppermute | solution.py:27
  83.4 0.2 broadcast_in_dim.8
  83.6 0.0 copy-done
  83.7 2.6 %collective-permute-done = f32[16,2048]{1,0:T(8,128)S(1)} collective-permute-done((f32[16,2048]{1,0:T(8,128)S(1)}, f32[16,2048]{1,0:T(8,128)S(1)}, u32[]{:S(2)}, u32[]{:S(2)}) %collective-permute-start) | collective-permute-done | bytes 131104 | tf_op jit(solution)/shard_map/ppermute | solution.py:22
  86.3 0.0 collective-permute-start.2
  86.3 0.0 collective-permute-done.1
  86.3 5.3 %collective-permute-start.3 = (f32[16,2048]{1,0:T(8,128)S(1)}, f32[16,2048]{1,0:T(8,128)S(1)}, u32[]{:S(2)}, u32[]{:S(2)}) collective-permute-start(f32[16,2048]{1,0:T(8,128)S(1)} %collective-permute-done.1), channel_id=1, source_target_pairs={{0,15},{1,0},{2,1},{3,2},{4,3},{5,4},{6,5},{7,6},{8,7},{9,8},{10,9... | collective-permute-start | bytes 393224 | tf_op jit(solution)/shard_map/ppermute | solution.py:27
  91.7 2.9 %collective-permute-done.2 = f32[16,2048]{1,0:T(8,128)S(1)} collective-permute-done((f32[16,2048]{1,0:T(8,128)S(1)}, f32[16,2048]{1,0:T(8,128)S(1)}, u32[]{:S(2)}, u32[]{:S(2)}) %collective-permute-start.2) | collective-permute-done | bytes 131104 | tf_op jit(solution)/shard_map/ppermute | solution.py:22
  94.6 0.0 collective-permute-start.4
  94.6 0.0 collective-permute-done.3
  94.6 5.3 %collective-permute-start.5 = (f32[16,2048]{1,0:T(8,128)S(1)}, f32[16,2048]{1,0:T(8,128)S(1)}, u32[]{:S(2)}, u32[]{:S(2)}) collective-permute-start(f32[16,2048]{1,0:T(8,128)S(1)} %collective-permute-done.3), channel_id=1, source_target_pairs={{0,15},{1,0},{2,1},{3,2},{4,3},{5,4},{6,5},{7,6},{8,7},{9,8},{10,9... | collective-permute-start | bytes 393224 | tf_op jit(solution)/shard_map/ppermute | solution.py:27
  100.0 3.6 %collective-permute-done.4 = f32[16,2048]{1,0:T(8,128)S(1)} collective-permute-done((f32[16,2048]{1,0:T(8,128)S(1)}, f32[16,2048]{1,0:T(8,128)S(1)}, u32[]{:S(2)}, u32[]{:S(2)}) %collective-permute-start.4) | collective-permute-done | bytes 131104 | tf_op jit(solution)/shard_map/ppermute | solution.py:22
  103.6 0.0 collective-permute-start.6
  103.6 0.0 collective-permute-done.5
  103.6 5.7 %collective-permute-start.7 = (f32[16,2048]{1,0:T(8,128)S(1)}, f32[16,2048]{1,0:T(8,128)S(1)}, u32[]{:S(2)}, u32[]{:S(2)}) collective-permute-start(f32[16,2048]{1,0:T(8,128)S(1)} %collective-permute-done.5), channel_id=1, source_target_pairs={{0,15},{1,0},{2,1},{3,2},{4,3},{5,4},{6,5},{7,6},{8,7},{9,8},{10,9... | collective-permute-start | bytes 393224 | tf_op jit(solution)/shard_map/ppermute | solution.py:27
  109.3 3.5 %collective-permute-done.6 = f32[16,2048]{1,0:T(8,128)S(1)} collective-permute-done((f32[16,2048]{1,0:T(8,128)S(1)}, f32[16,2048]{1,0:T(8,128)S(1)}, u32[]{:S(2)}, u32[]{:S(2)}) %collective-permute-start.6) | collective-permute-done | bytes 131104 | tf_op jit(solution)/shard_map/ppermute | solution.py:22
  112.8 0.0 collective-permute-start.8
  112.8 0.0 collective-permute-done.7
  112.8 5.3 %collective-permute-start.9 = (f32[16,2048]{1,0:T(8,128)S(1)}, f32[16,2048]{1,0:T(8,128)S(1)}, u32[]{:S(2)}, u32[]{:S(2)}) collective-permute-start(f32[16,2048]{1,0:T(8,128)S(1)} %collective-permute-done.7), channel_id=1, source_target_pairs={{0,15},{1,0},{2,1},{3,2},{4,3},{5,4},{6,5},{7,6},{8,7},{9,8},{10,9... | collective-permute-start | bytes 393224 | tf_op jit(solution)/shard_map/ppermute | solution.py:27
  118.2 3.1 %collective-permute-done.8 = f32[16,2048]{1,0:T(8,128)S(1)} collective-permute-done((f32[16,2048]{1,0:T(8,128)S(1)}, f32[16,2048]{1,0:T(8,128)S(1)}, u32[]{:S(2)}, u32[]{:S(2)}) %collective-permute-start.8) | collective-permute-done | bytes 131104 | tf_op jit(solution)/shard_map/ppermute | solution.py:22
  121.3 0.0 collective-permute-start.10
  121.3 0.0 collective-permute-done.9
  121.3 5.3 %collective-permute-start.11 = (f32[16,2048]{1,0:T(8,128)S(1)}, f32[16,2048]{1,0:T(8,128)S(1)}, u32[]{:S(2)}, u32[]{:S(2)}) collective-permute-start(f32[16,2048]{1,0:T(8,128)S(1)} %collective-permute-done.9), channel_id=1, source_target_pairs={{0,15},{1,0},{2,1},{3,2},{4,3},{5,4},{6,5},{7,6},{8,7},{9,8},{10,9... | collective-permute-start | bytes 393224 | tf_op jit(solution)/shard_map/ppermute | solution.py:27
  126.7 2.9 %collective-permute-done.10 = f32[16,2048]{1,0:T(8,128)S(1)} collective-permute-done((f32[16,2048]{1,0:T(8,128)S(1)}, f32[16,2048]{1,0:T(8,128)S(1)}, u32[]{:S(2)}, u32[]{:S(2)}) %collective-permute-start.10) | collective-permute-done | bytes 131104 | tf_op jit(solution)/shard_map/ppermute | solution.py:22
  129.6 0.0 collective-permute-start.12
  129.6 0.0 collective-permute-done.11
  129.6 5.3 %collective-permute-start.13 = (f32[16,2048]{1,0:T(8,128)S(1)}, f32[16,2048]{1,0:T(8,128)S(1)}, u32[]{:S(2)}, u32[]{:S(2)}) collective-permute-start(f32[16,2048]{1,0:T(8,128)S(1)} %collective-permute-done.11), channel_id=1, source_target_pairs={{0,15},{1,0},{2,1},{3,2},{4,3},{5,4},{6,5},{7,6},{8,7},{9,8},{10,9... | collective-permute-start | bytes 393224 | tf_op jit(solution)/shard_map/ppermute | solution.py:27
  135.0 2.9 %collective-permute-done.12 = f32[16,2048]{1,0:T(8,128)S(1)} collective-permute-done((f32[16,2048]{1,0:T(8,128)S(1)}, f32[16,2048]{1,0:T(8,128)S(1)}, u32[]{:S(2)}, u32[]{:S(2)}) %collective-permute-start.12) | collective-permute-done | bytes 131104 | tf_op jit(solution)/shard_map/ppermute | solution.py:22
  137.8 0.0 collective-permute-start.14
  137.9 0.0 collective-permute-done.13
  137.9 8.2 %collective-permute-done.14 = f32[16,2048]{1,0:T(8,128)S(1)} collective-permute-done((f32[16,2048]{1,0:T(8,128)S(1)}, f32[16,2048]{1,0:T(8,128)S(1)}, u32[]{:S(2)}, u32[]{:S(2)}) %collective-permute-start.14) | collective-permute-done | bytes 131104 | tf_op jit(solution)/shard_map/ppermute | solution.py:22
  146.2 1.5 fusion.7
  (19 shorter events, 0.3 us)
Async XLA Ops:
  6.5 70.4 %reduce-scatter.2.cloned.1.call-start = ((), (), s32[]{:S(2)}) async-start(), calls=%async_computation.1 | async-start | bytes 2228224 | tf_op jit(solution)/shard_map/reduce_scatter | solution.py:58
  13.7 2.8 %copy-start.1 = (s32[256]{0:T(256)S(1)}, s32[256]{0:T(256)}, u32[]{:S(2)}) copy-start(s32[256]{0:T(256)} %param.13) | copy-start | bytes 3076
  76.9 6.7 %copy-start = (f32[16,16,128]{2,0,1:T(8,128)S(1)}, f32[16,16,128]{2,0,1:T(8,128)}, u32[]{:S(2)}) copy-start(f32[16,16,128]{2,0,1:T(8,128)} %reduce-scatter.2.cloned.1.call-done) | copy-start | bytes 393220
  77.9 8.4 %collective-permute-start = (f32[16,2048]{1,0:T(8,128)S(1)}, f32[16,2048]{1,0:T(8,128)S(1)}, u32[]{:S(2)}, u32[]{:S(2)}) collective-permute-start(f32[16,2048]{1,0:T(8,128)S(1)} %bitcast.23), channel_id=1, source_target_pairs={{0,1},{1,2},{2,3},{3,4},{4,5},{5,6},{6,7},{7,8},{8,9},{9,10},{10,1... | collective-permute-start | bytes 393224 | tf_op jit(solution)/shard_map/ppermute | solution.py:22
  79.5 6.8 %collective-permute-start.1 = (f32[16,2048]{1,0:T(8,128)S(1)}, f32[16,2048]{1,0:T(8,128)S(1)}, u32[]{:S(2)}, u32[]{:S(2)}) collective-permute-start(f32[16,2048]{1,0:T(8,128)S(1)} %bitcast.24), channel_id=1, source_target_pairs={{0,15},{1,0},{2,1},{3,2},{4,3},{5,4},{6,5},{7,6},{8,7},{9,8},{10,9... | collective-permute-start | bytes 393224 | tf_op jit(solution)/shard_map/ppermute | solution.py:27
  86.3 8.3 %collective-permute-start.2 = (f32[16,2048]{1,0:T(8,128)S(1)}, f32[16,2048]{1,0:T(8,128)S(1)}, u32[]{:S(2)}, u32[]{:S(2)}) collective-permute-start(f32[16,2048]{1,0:T(8,128)S(1)} %collective-permute-done), channel_id=1, source_target_pairs={{0,1},{1,2},{2,3},{3,4},{4,5},{5,6},{6,7},{7,8},{8,9},{9,10},{10,1... | collective-permute-start | bytes 393224 | tf_op jit(solution)/shard_map/ppermute | solution.py:22
  86.3 8.3 %collective-permute-start.3 = (f32[16,2048]{1,0:T(8,128)S(1)}, f32[16,2048]{1,0:T(8,128)S(1)}, u32[]{:S(2)}, u32[]{:S(2)}) collective-permute-start(f32[16,2048]{1,0:T(8,128)S(1)} %collective-permute-done.1), channel_id=1, source_target_pairs={{0,15},{1,0},{2,1},{3,2},{4,3},{5,4},{6,5},{7,6},{8,7},{9,8},{10,9... | collective-permute-start | bytes 393224 | tf_op jit(solution)/shard_map/ppermute | solution.py:27
  94.6 9.0 %collective-permute-start.4 = (f32[16,2048]{1,0:T(8,128)S(1)}, f32[16,2048]{1,0:T(8,128)S(1)}, u32[]{:S(2)}, u32[]{:S(2)}) collective-permute-start(f32[16,2048]{1,0:T(8,128)S(1)} %collective-permute-done.2), channel_id=1, source_target_pairs={{0,1},{1,2},{2,3},{3,4},{4,5},{5,6},{6,7},{7,8},{8,9},{9,10},{10,1... | collective-permute-start | bytes 393224 | tf_op jit(solution)/shard_map/ppermute | solution.py:22
  94.6 9.0 %collective-permute-start.5 = (f32[16,2048]{1,0:T(8,128)S(1)}, f32[16,2048]{1,0:T(8,128)S(1)}, u32[]{:S(2)}, u32[]{:S(2)}) collective-permute-start(f32[16,2048]{1,0:T(8,128)S(1)} %collective-permute-done.3), channel_id=1, source_target_pairs={{0,15},{1,0},{2,1},{3,2},{4,3},{5,4},{6,5},{7,6},{8,7},{9,8},{10,9... | collective-permute-start | bytes 393224 | tf_op jit(solution)/shard_map/ppermute | solution.py:27
  103.6 9.2 %collective-permute-start.6 = (f32[16,2048]{1,0:T(8,128)S(1)}, f32[16,2048]{1,0:T(8,128)S(1)}, u32[]{:S(2)}, u32[]{:S(2)}) collective-permute-start(f32[16,2048]{1,0:T(8,128)S(1)} %collective-permute-done.4), channel_id=1, source_target_pairs={{0,1},{1,2},{2,3},{3,4},{4,5},{5,6},{6,7},{7,8},{8,9},{9,10},{10,1... | collective-permute-start | bytes 393224 | tf_op jit(solution)/shard_map/ppermute | solution.py:22
  103.6 9.2 %collective-permute-start.7 = (f32[16,2048]{1,0:T(8,128)S(1)}, f32[16,2048]{1,0:T(8,128)S(1)}, u32[]{:S(2)}, u32[]{:S(2)}) collective-permute-start(f32[16,2048]{1,0:T(8,128)S(1)} %collective-permute-done.5), channel_id=1, source_target_pairs={{0,15},{1,0},{2,1},{3,2},{4,3},{5,4},{6,5},{7,6},{8,7},{9,8},{10,9... | collective-permute-start | bytes 393224 | tf_op jit(solution)/shard_map/ppermute | solution.py:27
  112.8 8.4 %collective-permute-start.8 = (f32[16,2048]{1,0:T(8,128)S(1)}, f32[16,2048]{1,0:T(8,128)S(1)}, u32[]{:S(2)}, u32[]{:S(2)}) collective-permute-start(f32[16,2048]{1,0:T(8,128)S(1)} %collective-permute-done.6), channel_id=1, source_target_pairs={{0,1},{1,2},{2,3},{3,4},{4,5},{5,6},{6,7},{7,8},{8,9},{9,10},{10,1... | collective-permute-start | bytes 393224 | tf_op jit(solution)/shard_map/ppermute | solution.py:22
  112.8 8.4 %collective-permute-start.9 = (f32[16,2048]{1,0:T(8,128)S(1)}, f32[16,2048]{1,0:T(8,128)S(1)}, u32[]{:S(2)}, u32[]{:S(2)}) collective-permute-start(f32[16,2048]{1,0:T(8,128)S(1)} %collective-permute-done.7), channel_id=1, source_target_pairs={{0,15},{1,0},{2,1},{3,2},{4,3},{5,4},{6,5},{7,6},{8,7},{9,8},{10,9... | collective-permute-start | bytes 393224 | tf_op jit(solution)/shard_map/ppermute | solution.py:27
  121.3 8.3 %collective-permute-start.10 = (f32[16,2048]{1,0:T(8,128)S(1)}, f32[16,2048]{1,0:T(8,128)S(1)}, u32[]{:S(2)}, u32[]{:S(2)}) collective-permute-start(f32[16,2048]{1,0:T(8,128)S(1)} %collective-permute-done.8), channel_id=1, source_target_pairs={{0,1},{1,2},{2,3},{3,4},{4,5},{5,6},{6,7},{7,8},{8,9},{9,10},{10,1... | collective-permute-start | bytes 393224 | tf_op jit(solution)/shard_map/ppermute | solution.py:22
  121.3 8.3 %collective-permute-start.11 = (f32[16,2048]{1,0:T(8,128)S(1)}, f32[16,2048]{1,0:T(8,128)S(1)}, u32[]{:S(2)}, u32[]{:S(2)}) collective-permute-start(f32[16,2048]{1,0:T(8,128)S(1)} %collective-permute-done.9), channel_id=1, source_target_pairs={{0,15},{1,0},{2,1},{3,2},{4,3},{5,4},{6,5},{7,6},{8,7},{9,8},{10,9... | collective-permute-start | bytes 393224 | tf_op jit(solution)/shard_map/ppermute | solution.py:27
  129.6 8.3 %collective-permute-start.12 = (f32[16,2048]{1,0:T(8,128)S(1)}, f32[16,2048]{1,0:T(8,128)S(1)}, u32[]{:S(2)}, u32[]{:S(2)}) collective-permute-start(f32[16,2048]{1,0:T(8,128)S(1)} %collective-permute-done.10), channel_id=1, source_target_pairs={{0,1},{1,2},{2,3},{3,4},{4,5},{5,6},{6,7},{7,8},{8,9},{9,10},{10,1... | collective-permute-start | bytes 393224 | tf_op jit(solution)/shard_map/ppermute | solution.py:22
  129.6 8.3 %collective-permute-start.13 = (f32[16,2048]{1,0:T(8,128)S(1)}, f32[16,2048]{1,0:T(8,128)S(1)}, u32[]{:S(2)}, u32[]{:S(2)}) collective-permute-start(f32[16,2048]{1,0:T(8,128)S(1)} %collective-permute-done.11), channel_id=1, source_target_pairs={{0,15},{1,0},{2,1},{3,2},{4,3},{5,4},{6,5},{7,6},{8,7},{9,8},{10,9... | collective-permute-start | bytes 393224 | tf_op jit(solution)/shard_map/ppermute | solution.py:27
  137.8 8.3 %collective-permute-start.14 = (f32[16,2048]{1,0:T(8,128)S(1)}, f32[16,2048]{1,0:T(8,128)S(1)}, u32[]{:S(2)}, u32[]{:S(2)}) collective-permute-start(f32[16,2048]{1,0:T(8,128)S(1)} %collective-permute-done.12), channel_id=1, source_target_pairs={{0,1},{1,2},{2,3},{3,4},{4,5},{5,6},{6,7},{7,8},{8,9},{9,10},{10,1... | collective-permute-start | bytes 393224 | tf_op jit(solution)/shard_map/ppermute | solution.py:22
Sparse Core Ops, SparseCore 0:
  16.3 60.5 reduce-scatter.1
